TPU v7x, 32 devices: a whole 2x2x4 slice. The times are simulated.
32 devices in a mesh: groups: 2 (over y), row: 8 (over z, x), col: 2 (over core).
Axes of the slice: x: 2, y: 2, z: 4, core: 2. Of those that a mesh axis runs over, the one named last changes fastest.
Arguments:
- inputs: bfloat16 [32, 8192], P(('groups', 'row'), 'col'), parts along dimension 0, may hold values from -6 to 6
- out_grads: bfloat16 [32, 8192], P(('groups', 'row'), 'col'), parts along dimension 0, may hold values from -6 to 6
- w_gate: bfloat16 [8192, 24576], P('col', 'row'), may hold values from -0.0625 to 0.0625
- w_up: bfloat16 [8192, 24576], P('col', 'row'), may hold values from -0.0625 to 0.0625
- w_down: bfloat16 [24576, 8192], P('row', 'col'), may hold values from -0.0390625 to 0.0390625
Outputs:
- attribution: float32 [32, 8192], P(('groups', 'row'), 'col'), parts along dimension 0
There are 2 independent parts, one for each index of `groups`. A program takes and returns all parts, laid end to end along the dimension named above; an argument that names none is the same for every part. Nothing has to cross between parts.
All inputs are finite; a program needn't handle non-finite values.
Results may differ from a plain program's by a relative error of at most 0.0029.
Values may be sent and summed in bfloat16 or wider, within the bound.
A program may use at most 192 MiB of HBM per device.

v0:
```python
import jax
import jax.numpy as jnp
from jax import lax
from jax.sharding import PartitionSpec as P


def derivatives(sums):
    gated = sums[0]
    upward = sums[1]
    backward = sums[2]
    sigma = jax.nn.sigmoid(gated)
    grad_gate = (backward * upward * sigma * (1.0 + gated * (1.0 - sigma))).astype(jnp.bfloat16)
    grad_up = (backward * gated * sigma).astype(jnp.bfloat16)
    return jnp.stack([grad_gate, grad_up])


def per_device(inputs, out_grads, w_gate, w_up, w_down):
    stacked = jnp.stack([inputs, out_grads])
    piece = lax.all_gather(stacked, "row", axis=1, tiled=True)
    gated = jnp.dot(piece[0], w_gate, preferred_element_type=jnp.float32)
    upward = jnp.dot(piece[0], w_up, preferred_element_type=jnp.float32)
    backward = lax.dot_general(
        piece[1], w_down, (((1,), (1,)), ((), ())), preferred_element_type=jnp.float32
    )
    partial_sums = jnp.stack([gated, upward, backward])
    summed = lax.psum(partial_sums, "col")
    derived = derivatives(summed)
    total = lax.dot_general(
        derived[0], w_gate, (((1,), (1,)), ((), ())), preferred_element_type=jnp.float32
    )
    grad_input = lax.psum_scatter(
        total
        + lax.dot_general(
            derived[1], w_up, (((1,), (1,)), ((), ())), preferred_element_type=jnp.float32
        ),
        "row",
        scatter_dimension=0,
        tiled=True,
    )
    return inputs.astype(jnp.float32) * grad_input


def solution(mesh):
    in_specs = (
        P(("groups", "row"), "col"),
        P(("groups", "row"), "col"),
        P("col", "row"),
        P("col", "row"),
        P("row", "col"),
    )
    out_specs = P(("groups", "row"), "col")
    return jax.shard_map(
        per_device, mesh=mesh, in_specs=in_specs, out_specs=out_specs, check_vma=False
    )
```

profile of v0, /device:TPU:0, one launch (start us, length us, event | category | flops | bytes accessed | tf_op | source)
XLA Modules:
  0.0 200.1 jit_solution(14004625171131348486)
XLA Ops:
  6.5 0.0 all-reduce.4.cloned.1.call-start
  6.5 0.8 pad_maximum_fusion.1
  7.4 32.5 %all_gather.3 = bf16[2,16,4096]{2,0,1:T(2,128)(2,1)S(1)} all-gather(bf16[2,2,4096]{2,0,1:T(2,128)(2,1)S(1)} %copy.6), channel_id=1, replica_groups=mesh['groups'=2,'row'=8,'col'=2] {'row'}, dimensions={1}, use_global_device_ids=true | all-gather | bytes 294912 | tf_op jit(solution)/shard_map/all_gather | solution.py:19
  39.9 0.4 fusion.10
  40.3 10.0 %convolution_bitcast_fusion.1 = f32[1,16,3072]{2,1,0:T(8,128)S(1)} fusion(bf16[4096,3072]{1,0:T(8,128)(2,1)} %param.8, bf16[1,16,4096]{2,0,1:T(2,128)(2,1)S(1)} %get-tuple-element.5), kind=kOutput, calls=%fused_computation.2 | convolution fusion | flops 402653184 | bytes 25493504 | tf_op jit(solution)/shard_map/dot_general | solution.py:21
  50.2 10.0 %convolution_bitcast_fusion.2 = f32[1,16,3072]{2,1,0:T(8,128)S(1)} fusion(bf16[4096,3072]{1,0:T(8,128)(2,1)} %param.7, bf16[1,16,4096]{2,0,1:T(2,128)(2,1)S(1)} %get-tuple-element.5), kind=kOutput, calls=%fused_computation.3 | convolution fusion | flops 402653184 | bytes 25493504 | tf_op jit(solution)/shard_map/dot_general | solution.py:20
  60.2 11.5 %convolution_bitcast_fusion = f32[1,16,3072]{2,1,0:T(8,128)S(1)} fusion(bf16[3072,4096]{1,0:T(8,128)(2,1)} %param.9, bf16[1,16,4096]{2,0,1:T(2,128)(2,1)S(1)} %get-tuple-element.6), kind=kOutput, calls=%fused_computation.1 | convolution fusion | flops 402653184 | bytes 25493504 | tf_op jit(solution)/shard_map/dot_general | solution.py:22
  71.7 0.9 pad_maximum_fusion
  72.6 0.0 all-reduce.4.cloned.1.call-update
  72.6 0.0 all-reduce.6.cloned.1.call-start
  72.7 19.9 %all-reduce.4.cloned.1.call-done = f32[3,16,3072]{2,1,0:T(8,128)} async-done(((f32[3,16,3072]{2,1,0:T(8,128)}), f32[3,16,3072]{2,1,0:T(8,128)}) %all-reduce.4.cloned.1.call-update) | async-done | bytes 589840 | tf_op jit(solution)/shard_map/psum | solution.py:26
  92.6 0.0 copy-start
  92.6 14.9 %fusion.4 = f32[16,4096]{1,0:T(8,128)S(1)} fusion(bf16[4096,3072]{1,0:T(8,128)(2,1)} %param.7, f32[3,16,3072]{2,1,0:T(8,128)} %all-reduce.4.cloned.1.call-done), kind=kOutput, calls=%fused_computation.16 | convolution fusion | flops 403144704 | bytes 26017792 | tf_op jit(solution)/shard_map/dot_general | solution.py:28
  107.5 0.0 copy-done
  107.5 0.0 copy-start.2
  107.5 0.0 copy-start.1
  107.5 12.3 %convolution_add_fusion = f32[16,4096]{1,0:T(8,128)} fusion(f32[16,4096]{1,0:T(8,128)S(1)} %fusion.4, bf16[4096,3072]{1,0:T(8,128)(2,1)} %param.8, f32[3,16,3072]{2,1,0:T(8,128)S(1)} %copy-done), kind=kOutput, calls=%fused_computation | convolution fusion | flops 403013632 | bytes 26083328 | tf_op jit(solution)/shard_map/dot_general | solution.py:33
  119.8 0.0 all-reduce.6.cloned.1.call-update
  119.8 0.0 copy-done.2
  119.8 0.6 dynamic-slice
  121.1 70.6 %all-reduce.6.cloned.1.call-done = f32[16,4096]{1,0:T(8,128)} async-done(((f32[16,4096]{1,0:T(8,128)}), f32[16,4096]{1,0:T(8,128)}) %all-reduce.6.cloned.1.call-update) | async-done | bytes 262160
  191.7 0.0 copy-done.1
  191.7 1.5 dynamic-slice_multiply_fusion
  (1 shorter events, 0.0 us)
Async XLA Ops:
  6.5 86.1 %all-reduce.4.cloned.1.call-start = ((), (), s32[]{:S(2)}) async-start(), calls=%async_computation | async-start | bytes 1179648 | tf_op jit(solution)/shard_map/psum | solution.py:26
  72.6 119.1 %all-reduce.6.cloned.1.call-start = ((), (), s32[]{:S(2)}) async-start(), calls=%async_computation.1 | async-start | bytes 524288
  92.6 14.9 %copy-start = (f32[3,16,3072]{2,1,0:T(8,128)S(1)}, f32[3,16,3072]{2,1,0:T(8,128)}, u32[]{:S(2)}) copy-start(f32[3,16,3072]{2,1,0:T(8,128)} %all-reduce.4.cloned.1.call-done) | copy-start | bytes 1769476
  107.5 12.3 %copy-start.2 = (u32[32]{0:T(128)S(1)}, u32[32]{0:T(128)}, u32[]{:S(2)}) copy-start(u32[32]{0:T(128)} %constant.6) | copy-start | bytes 388
  107.5 84.2 %copy-start.1 = (bf16[2,4096]{1,0:T(2,128)(2,1)S(1)}, bf16[2,4096]{1,0:T(2,128)(2,1)}, u32[]{:S(2)}) copy-start(bf16[2,4096]{1,0:T(2,128)(2,1)} %param.5) | copy-start | bytes 49156
Sparse Core Ops, SparseCore 0:
  72.8 19.7 all-reduce.3
  119.9 71.7 all-reduce.5
where the time goes:
time: 200 us
  waiting for transfers between devices  90.6 us (45%)
  matrix products  58.6 us (29%)
  blocking collectives  32.5 us (16%)
  between operations  14.1 us (7%)
  other arithmetic  3.21 us (2%)
    unnamed x3, waiting for transfers between devices  70.7 us
    all_gather x1, blocking collectives, per_device(): piece = lax.all_gather(stacked, 'row', axis=1, tiled=True)  32.5 us
    psum x1, waiting for transfers between devices, per_device(): summed = lax.psum(partial_sums, 'col')  19.9 us
    dot_general x1, matrix products, per_device(): lax.dot_general(derived[0], w_gate, (((1,), (1,)), ((), ())), preferred_e...  14.9 us
    dot_general x1, matrix products, per_device(): lax.dot_general(derived[1], w_up, (((1,), (1,)), ((), ())), preferred_ele...  12.3 us
    dot_general x1, matrix products, per_device(): lax.dot_general(piece[1], w_down, (((1,), (1,)), ((), ())), preferred_ele...  11.5 us
    dot_general x1, matrix products, per_device(): gated = jnp.dot(piece[0], w_gate, preferred_element_type=jnp.float32)  9.97 us
    dot_general x1, matrix products, per_device(): upward = jnp.dot(piece[0], w_up, preferred_element_type=jnp.float32)  9.97 us
  transfers between devices with their start and end apart: 2, of which 2 were waited for; matrix products, arithmetic and copies ran while one was open for 0% of the time, Pallas kernels for 0%

commit v1 on v0

v1 whole, which is shorter than its diff:
```python
import functools

import jax
import jax.numpy as jnp
from jax import lax
from jax.experimental import pallas as pl
from jax.experimental.pallas import tpu as pltpu
from jax.sharding import PartitionSpec as P

MESH = pl.DeviceIdType.MESH
TILE = 256
NT = (((1,), (1,)), ((), ()))


def derivatives(sums):
    gated = sums[0]
    upward = sums[1]
    backward = sums[2]
    sigma = jax.nn.sigmoid(gated)
    grad_gate = (backward * upward * sigma * (1.0 + gated * (1.0 - sigma))).astype(jnp.bfloat16)
    grad_up = (backward * gated * sigma).astype(jnp.bfloat16)
    return jnp.stack([grad_gate, grad_up])


def per_device(inputs, out_grads, w_gate, w_up, w_down):
    stacked = jnp.stack([inputs, out_grads])
    piece = lax.all_gather(stacked, "row", axis=1, tiled=True)
    gated = jnp.dot(piece[0], w_gate, preferred_element_type=jnp.float32)
    upward = jnp.dot(piece[0], w_up, preferred_element_type=jnp.float32)
    backward = lax.dot_general(piece[1], w_down, NT, preferred_element_type=jnp.float32)
    partial_sums = jnp.stack([gated, upward, backward])
    summed = lax.psum(partial_sums, "col")
    derived = derivatives(summed)
    total = lax.dot_general(derived[0], w_gate, NT, preferred_element_type=jnp.float32)
    grad_input = lax.psum_scatter(
        total + lax.dot_general(derived[1], w_up, NT, preferred_element_type=jnp.float32),
        "row",
        scatter_dimension=0,
        tiled=True,
    )
    return inputs.astype(jnp.float32) * grad_input


def kernel(
    nz, tiles,
    in_hbm, og_hbm, wg_hbm, wu_hbm, wd_hbm, out_ref,
    wg, wu, wd, gx, gy, stage, xs, ys, part, peer, acc, own, s1, r1, mid, s2, r2,
    w_sem, l_sem, z_send, z_recv, p_send, p_recv, c_send, c_recv,
    a_send, a_recv, b_send, b_recv,
):
    tokens, feats = in_hbm.shape
    rows = nz * tokens
    half = tiles * TILE
    g = lax.axis_index("groups")
    r = lax.axis_index("row")
    c = lax.axis_index("col")
    x = lax.rem(r, 2)
    z = r // 2
    plane = g * 2 + x

    def z_dev(d):
        return {"row": lax.rem(z + d, nz) * 2 + x}

    def p_index(d):
        return lax.rem(plane + d, 4)

    def p_dev(d):
        q = lax.rem(plane + d, 4)
        return {"groups": q // 2, "row": z * 2 + lax.rem(q, 2)}

    def weight_copies(j):
        at = pl.multiple_of(g * half + j * TILE, TILE)
        return (
            pltpu.make_async_copy(wg_hbm.at[:, pl.ds(at, TILE)], wg.at[j], w_sem.at[0, j]),
            pltpu.make_async_copy(wu_hbm.at[:, pl.ds(at, TILE)], wu.at[j], w_sem.at[1, j]),
            pltpu.make_async_copy(wd_hbm.at[pl.ds(at, TILE), :], wd.at[j], w_sem.at[2, j]),
        )

    own_x = pltpu.make_async_copy(in_hbm, gx.at[plane, z], l_sem.at[0])
    own_y = pltpu.make_async_copy(og_hbm, gy.at[plane, z], l_sem.at[1])
    own_x.start()
    own_y.start()

    @pl.loop(0, tiles)
    def _(j):
        for copy in weight_copies(j):
            copy.start()

    barrier = pltpu.get_barrier_semaphore()
    for d in range(1, nz):
        pl.semaphore_signal(barrier, inc=1, device_id=z_dev(d), device_id_type=MESH)
    for d in range(1, 4):
        pl.semaphore_signal(barrier, inc=1, device_id=p_dev(d), device_id_type=MESH)
    pl.semaphore_signal(barrier, inc=1, device_id={"col": 1 - c}, device_id_type=MESH)
    pl.semaphore_wait(barrier, nz + 3)

    sources = ((in_hbm, gx), (og_hbm, gy))
    z_copies = [
        [
            pltpu.make_async_remote_copy(
                src_ref=src, dst_ref=buf.at[plane, z],
                send_sem=z_send.at[a, d - 1], recv_sem=z_recv.at[a, d - 1],
                device_id=z_dev(d), device_id_type=MESH,
            )
            for d in range(1, nz)
        ]
        for a, (src, buf) in enumerate(sources)
    ]
    p_copies = [
        [
            pltpu.make_async_remote_copy(
                src_ref=buf.at[plane], dst_ref=buf.at[plane],
                send_sem=p_send.at[a, d - 1], recv_sem=p_recv.at[a, d - 1],
                device_id=p_dev(d), device_id_type=MESH,
            )
            for d in range(1, 4)
        ]
        for a, (_, buf) in enumerate(sources)
    ]
    for a in range(2):
        for copy in z_copies[a]:
            copy.start()
    for a, local in enumerate((own_x, own_y)):
        local.wait()
        for copy in z_copies[a]:
            copy.wait_recv()
        for copy in p_copies[a]:
            copy.start()

    def arrange(a, buf, dst):
        for copy in p_copies[a]:
            copy.wait_recv()
        for q in range(4):
            for k in range(nz):
                at = q * rows + k * tokens
                stage[at:at + tokens, :] = buf[q, k].astype(jnp.float32)
        dst[...] = stage[...].astype(jnp.bfloat16)

    arrange(0, gx, xs)
    arrange(1, gy, ys)
    acc[...] = jnp.zeros_like(acc)

    def exchange(j):
        return pltpu.make_async_remote_copy(
            src_ref=part.at[j], dst_ref=peer.at[j],
            send_sem=c_send.at[j], recv_sem=c_recv.at[j],
            device_id={"col": 1 - c}, device_id_type=MESH,
        )

    def forward(j):
        gate, up, down = weight_copies(j)
        gate.wait()
        part[j, 0] = jnp.dot(xs[...], wg[j], preferred_element_type=jnp.float32)
        up.wait()
        part[j, 1] = jnp.dot(xs[...], wu[j], preferred_element_type=jnp.float32)
        down.wait()
        part[j, 2] = lax.dot_general(ys[...], wd[j], NT, preferred_element_type=jnp.float32)
        exchange(j).start()

    def finish(j):
        exchange(j).wait_recv()
        gated = part[j, 0] + peer[j, 0]
        upward = part[j, 1] + peer[j, 1]
        backward = part[j, 2] + peer[j, 2]
        sigma = 1.0 / (1.0 + jnp.exp(-gated))
        gate = (backward * upward * sigma * (1.0 + gated * (1.0 - sigma))).astype(jnp.bfloat16)
        up = (backward * gated * sigma).astype(jnp.bfloat16)
        acc[...] += lax.dot_general(
            gate, wg[j], NT, preferred_element_type=jnp.float32
        ) + lax.dot_general(up, wu[j], NT, preferred_element_type=jnp.float32)

    @pl.loop(0, tiles + 1)
    def _(j):
        @pl.when(j < tiles)
        def _():
            forward(j)

        @pl.when(j > 0)
        def _():
            finish(j - 1)

    for q in range(4):
        s1[q] = acc[q * rows:(q + 1) * rows, :].astype(jnp.bfloat16)
    a_copies = [
        pltpu.make_async_remote_copy(
            src_ref=s1.at[p_index(d)], dst_ref=r1.at[d - 1],
            send_sem=a_send.at[d - 1], recv_sem=a_recv.at[d - 1],
            device_id=p_dev(d), device_id_type=MESH,
        )
        for d in range(1, 4)
    ]
    for copy in a_copies:
        copy.start()
    own[...] = acc[pl.ds(pl.multiple_of(plane * rows, rows), rows), :]
    for copy in a_copies:
        copy.wait_recv()
    own[...] = own[...] + r1[0].astype(jnp.float32) + r1[1].astype(jnp.float32) + r1[2].astype(jnp.float32)
    for k in range(nz):
        mid[k] = own[k * tokens:(k + 1) * tokens, :]
        s2[k] = mid[k].astype(jnp.bfloat16)
    b_copies = [
        pltpu.make_async_remote_copy(
            src_ref=s2.at[lax.rem(z + d, nz)], dst_ref=r2.at[d - 1],
            send_sem=b_send.at[d - 1], recv_sem=b_recv.at[d - 1],
            device_id=z_dev(d), device_id_type=MESH,
        )
        for d in range(1, nz)
    ]
    for copy in b_copies:
        copy.start()
    total = mid[z]
    for d in range(1, nz):
        b_copies[d - 1].wait_recv()
        total = total + r2[d - 1].astype(jnp.float32)
    out_ref[...] = gx[plane, z].astype(jnp.float32) * total

    for copies in z_copies + p_copies + [a_copies, b_copies]:
        for copy in copies:
            copy.wait_send()

    @pl.loop(0, tiles)
    def _(j):
        exchange(j).wait_send()


def shared(nz, inputs, out_grads, w_gate, w_up, w_down):
    tokens, feats = inputs.shape
    tiles = w_gate.shape[1] // (2 * TILE)
    rows = nz * tokens
    every = 4 * rows
    f32, bf16 = jnp.float32, jnp.bfloat16
    dma = pltpu.SemaphoreType.DMA
    return pl.pallas_call(
        functools.partial(kernel, nz, tiles),
        out_shape=jax.ShapeDtypeStruct((tokens, feats), f32),
        in_specs=[pl.BlockSpec(memory_space=pl.ANY)] * 5,
        out_specs=pl.BlockSpec(memory_space=pltpu.VMEM),
        scratch_shapes=[
            pltpu.VMEM((tiles, feats, TILE), bf16),
            pltpu.VMEM((tiles, feats, TILE), bf16),
            pltpu.VMEM((tiles, TILE, feats), bf16),
            pltpu.VMEM((4, nz, tokens, feats), bf16),
            pltpu.VMEM((4, nz, tokens, feats), bf16),
            pltpu.VMEM((every, feats), f32),
            pltpu.VMEM((every, feats), bf16),
            pltpu.VMEM((every, feats), bf16),
            pltpu.VMEM((tiles, 3, every, TILE), f32),
            pltpu.VMEM((tiles, 3, every, TILE), f32),
            pltpu.VMEM((every, feats), f32),
            pltpu.VMEM((rows, feats), f32),
            pltpu.VMEM((4, rows, feats), bf16),
            pltpu.VMEM((3, rows, feats), bf16),
            pltpu.VMEM((nz, tokens, feats), f32),
            pltpu.VMEM((nz, tokens, feats), bf16),
            pltpu.VMEM((nz - 1, tokens, feats), bf16),
            dma((3, tiles)), dma((2,)),
            dma((2, nz - 1)), dma((2, nz - 1)),
            dma((2, 3)), dma((2, 3)),
            dma((tiles,)), dma((tiles,)),
            dma((3,)), dma((3,)),
            dma((nz - 1,)), dma((nz - 1,)),
        ],
        compiler_params=pltpu.CompilerParams(
            collective_id=0, has_side_effects=True, vmem_limit_bytes=60 << 20
        ),
    )(inputs, out_grads, w_gate, w_up, w_down)


def solution(mesh):
    in_specs = (
        P(("groups", "row"), "col"),
        P(("groups", "row"), "col"),
        P("col", "row"),
        P("col", "row"),
        P("row", "col"),
    )
    out_specs = P(("groups", "row"), "col")
    groups, row, col = (mesh.shape[name] for name in ("groups", "row", "col"))

    def body(inputs, out_grads, w_gate, w_up, w_down):
        tokens, feats = inputs.shape
        nz = row // 2
        hidden = w_gate.shape[1]
        held = 3 * feats * hidden + 60 * groups * row * tokens * feats
        fits = (
            groups == 2 and col == 2 and row % 2 == 0 and nz > 1
            and hidden % (2 * TILE) == 0 and feats % TILE == 0
            and nz * tokens == 8 and held < (56 << 20)
        )
        plan = functools.partial(shared, nz) if fits else per_device
        return plan(inputs, out_grads, w_gate, w_up, w_down)

    return jax.shard_map(
        body, mesh=mesh, in_specs=in_specs, out_specs=out_specs, check_vma=False
    )
```

time: 200 us -> 48.2 us (0.24)
  waiting for transfers between devices: 90.6 us -> 0 us
  matrix products: 58.6 us -> 0 us
  Pallas kernels: 0 us -> 46.6 us
  blocking collectives: 32.5 us -> 0 us
  between operations: 14.1 us -> 0.01 us
  other arithmetic: 3.21 us -> 0 us
    unnamed x3 -> x0, waiting for transfers between devices: 70.7 us -> none
    dot_general x5 -> x0, matrix products: 58.6 us -> none  [the longest x1 14.9 us: per_device(): lax.dot_general(derived[0], w_gate, (((1,), (1,)), ((), ())), preferred_e...]
    pallas_call x0 -> x1, Pallas kernels: none -> 46.6 us  [shared(): pl.pallas_call(functools.partial(kernel, nz, tiles), out_shape=jax.ShapeD...]
    all_gather x1 -> x0, blocking collectives: 32.5 us -> none  [per_device(): piece = lax.all_gather(stacked, 'row', axis=1, tiled=True)]
    psum x1 -> x0, waiting for transfers between devices: 19.9 us -> none  [per_device(): summed = lax.psum(partial_sums, 'col')]
  transfers between devices with their start and end apart: 2 -> 0, of which waited for: 2 -> 0; matrix products, arithmetic and copies ran while one was open for 0% -> 0% of each run, Pallas kernels for 0% -> 0%
where the time goes in v1:
time: 48.2 us; the launch traced here: 48 us
  Pallas kernels  46.6 us (97%)
  local copies, waits for them, and re-layouts  1.38 us (3%)
    pallas_call x1, Pallas kernels, shared(): pl.pallas_call(functools.partial(kernel, nz, tiles), out_shape=jax.ShapeD...  46.6 us
    unnamed x1, local copies, waits for them, and re-layouts  1.38 us

profile of v1, /device:TPU:0, one launch (start us, length us, event | category | flops | bytes accessed | tf_op | source)
XLA Modules:
  0.0 48.0 jit_solution(6905455728847389415)
XLA Ops:
  0.0 46.6 %shard_map.55 = f32[2,4096]{1,0:T(2,128)} custom-call(bf16[2,4096]{1,0:T(2,128)(2,1)} %in_hbm.1, bf16[2,4096]{1,0:T(2,128)(2,1)} %og_hbm.1, bf16[4096,3072]{1,0:T(8,128)(2,1)} %wg_hbm.1, bf16[4096,3072]{1,0:T(8,128)(2,1)} %wu_hbm.1, bf16[3072,4096]{1,0:T(8,128)(2,1)} %wd_hbm.1), custom_call_target="tpu_custom_call" | custom-call | tf_op jit(solution)/shard_map/pallas_call | solution.py:233
  46.6 1.4 %copy.7 = f32[2,4096]{1,0:T(2,128)} copy(f32[2,4096]{1,0:T(2,128)} %shard_map.55) | data formatting | bytes 65536

commit v2 on v0

v2 whole, which is shorter than its diff:
```python
import functools

import jax
import jax.numpy as jnp
from jax import lax
from jax.experimental import pallas as pl
from jax.experimental.pallas import tpu as pltpu
from jax.sharding import PartitionSpec as P

MESH = pl.DeviceIdType.MESH
TILE = 512
CHUNKS = 4
NT = (((1,), (1,)), ((), ()))


def derivatives(sums):
    gated = sums[0]
    upward = sums[1]
    backward = sums[2]
    sigma = jax.nn.sigmoid(gated)
    grad_gate = (backward * upward * sigma * (1.0 + gated * (1.0 - sigma))).astype(jnp.bfloat16)
    grad_up = (backward * gated * sigma).astype(jnp.bfloat16)
    return jnp.stack([grad_gate, grad_up])


def per_device(inputs, out_grads, w_gate, w_up, w_down):
    stacked = jnp.stack([inputs, out_grads])
    piece = lax.all_gather(stacked, "row", axis=1, tiled=True)
    gated = jnp.dot(piece[0], w_gate, preferred_element_type=jnp.float32)
    upward = jnp.dot(piece[0], w_up, preferred_element_type=jnp.float32)
    backward = lax.dot_general(piece[1], w_down, NT, preferred_element_type=jnp.float32)
    partial_sums = jnp.stack([gated, upward, backward])
    summed = lax.psum(partial_sums, "col")
    derived = derivatives(summed)
    total = lax.dot_general(derived[0], w_gate, NT, preferred_element_type=jnp.float32)
    grad_input = lax.psum_scatter(
        total + lax.dot_general(derived[1], w_up, NT, preferred_element_type=jnp.float32),
        "row",
        scatter_dimension=0,
        tiled=True,
    )
    return inputs.astype(jnp.float32) * grad_input


def kernel(
    nz, tiles,
    in_hbm, og_hbm, wg_hbm, wu_hbm, wd_hbm, out_ref,
    wg, wu, wd, gx, gy, stage, xs, ys, part, peer, down, dpeer, dg, du, acc,
    s1, r1, mid, s2, r2,
    w_sem, l_sem, z_send, z_recv, p_send, p_recv, c_send, c_recv, d_send, d_recv,
    a_send, a_recv, b_send, b_recv,
):
    tokens, feats = in_hbm.shape
    rows = nz * tokens
    half = tiles * TILE
    width = feats // CHUNKS
    g = lax.axis_index("groups")
    r = lax.axis_index("row")
    c = lax.axis_index("col")
    x = lax.rem(r, 2)
    z = r // 2
    plane = g * 2 + x

    def z_dev(d):
        return {"row": lax.rem(z + d, nz) * 2 + x}

    def p_index(d):
        return lax.rem(plane + d, 4)

    def p_dev(d):
        q = lax.rem(plane + d, 4)
        return {"groups": q // 2, "row": z * 2 + lax.rem(q, 2)}

    def remote(src, dst, send, recv, device):
        return pltpu.make_async_remote_copy(
            src_ref=src, dst_ref=dst, send_sem=send, recv_sem=recv,
            device_id=device, device_id_type=MESH,
        )

    own = [
        pltpu.make_async_copy(in_hbm, gx.at[plane, z], l_sem.at[0]),
        pltpu.make_async_copy(og_hbm, gy.at[plane, z], l_sem.at[1]),
    ]
    for copy in own:
        copy.start()

    barrier = pltpu.get_barrier_semaphore()
    for d in range(1, nz):
        pl.semaphore_signal(barrier, inc=1, device_id=z_dev(d), device_id_type=MESH)
    for d in range(1, 4):
        pl.semaphore_signal(barrier, inc=1, device_id=p_dev(d), device_id_type=MESH)
    pl.semaphore_signal(barrier, inc=1, device_id={"col": 1 - c}, device_id_type=MESH)

    gates, ups, downs = [], [], []
    for j in range(tiles):
        at = pl.ds(pl.multiple_of(g * half + j * TILE, TILE), TILE)
        to = pl.ds(j * TILE, TILE)
        gates.append(pltpu.make_async_copy(wg_hbm.at[:, at], wg.at[:, to], w_sem.at[0, j]))
        ups.append(pltpu.make_async_copy(wu_hbm.at[:, at], wu.at[:, to], w_sem.at[1, j]))
        downs.append(pltpu.make_async_copy(wd_hbm.at[at, :], wd.at[to, :], w_sem.at[2, j]))
    for j in range(tiles):
        gates[j].start()
        ups[j].start()
    for j in range(tiles):
        downs[j].start()

    for copy in own:
        copy.wait()
    pl.semaphore_wait(barrier, nz + 3)

    buffers = (gx, gy)
    z_copies = [
        [
            remote(buf.at[plane, z], buf.at[plane, z], z_send.at[a, d - 1], z_recv.at[a, d - 1], z_dev(d))
            for d in range(1, nz)
        ]
        for a, buf in enumerate(buffers)
    ]
    p_copies = [
        [
            [
                remote(
                    buf.at[plane, lax.rem(z + nz - k, nz)], buf.at[plane, lax.rem(z + nz - k, nz)],
                    p_send.at[a, k, d - 1], p_recv.at[a, k, d - 1], p_dev(d),
                )
                for d in range(1, 4)
            ]
            for k in range(nz)
        ]
        for a, buf in enumerate(buffers)
    ]
    for copy in z_copies[0] + p_copies[0][0] + z_copies[1]:
        copy.start()
    for a in range(2):
        if a:
            for copy in p_copies[a][0]:
                copy.start()
        for k in range(1, nz):
            z_copies[a][k - 1].wait_recv()
            for copy in p_copies[a][k]:
                copy.start()

    def arrange(a, buf, dst):
        for copies in p_copies[a]:
            for copy in copies:
                copy.wait_recv()
        for q in range(4):
            for k in range(nz):
                at = q * rows + k * tokens
                stage[at:at + tokens, :] = buf[q, k].astype(jnp.float32)
        dst[...] = stage[...].astype(jnp.bfloat16)

    other = {"col": 1 - c}
    gu_moves = [remote(part.at[j], peer.at[j], c_send.at[j], c_recv.at[j], other) for j in range(tiles)]
    dn_moves = [remote(down.at[j], dpeer.at[j], d_send.at[j], d_recv.at[j], other) for j in range(tiles)]

    arrange(0, gx, xs)
    for j in range(tiles):
        cols = slice(j * TILE, (j + 1) * TILE)
        gates[j].wait()
        part[j, 0] = jnp.dot(xs[...], wg[:, cols], preferred_element_type=jnp.float32)
        ups[j].wait()
        part[j, 1] = jnp.dot(xs[...], wu[:, cols], preferred_element_type=jnp.float32)
        gu_moves[j].start()
    arrange(1, gy, ys)
    for j in range(tiles):
        downs[j].wait()
        down[j] = lax.dot_general(
            ys[...], wd[j * TILE:(j + 1) * TILE, :], NT, preferred_element_type=jnp.float32
        )
        dn_moves[j].start()

    def derive(j):
        gu_moves[j].wait_recv()
        dn_moves[j].wait_recv()
        gated = part[j, 0] + peer[j, 0]
        upward = part[j, 1] + peer[j, 1]
        backward = down[j] + dpeer[j]
        sigma = 1.0 / (1.0 + jnp.exp(-gated))
        cols = slice(j * TILE, (j + 1) * TILE)
        dg[:, cols] = (backward * upward * sigma * (1.0 + gated * (1.0 - sigma))).astype(jnp.bfloat16)
        du[:, cols] = (backward * gated * sigma).astype(jnp.bfloat16)

    def product(f, lo, hi):
        at = slice(f * width, (f + 1) * width)
        cols = slice(lo * TILE, hi * TILE)
        return lax.dot_general(
            dg[:, cols], wg[at, cols], NT, preferred_element_type=jnp.float32
        ) + lax.dot_general(du[:, cols], wu[at, cols], NT, preferred_element_type=jnp.float32)

    a_copies = [
        [
            remote(s1.at[f, p_index(d)], r1.at[f, d - 1], a_send.at[f, d - 1], a_recv.at[f, d - 1], p_dev(d))
            for d in range(1, 4)
        ]
        for f in range(CHUNKS)
    ]
    b_copies = [
        [
            remote(s2.at[f, lax.rem(z + d, nz)], r2.at[f, d - 1], b_send.at[f, d - 1], b_recv.at[f, d - 1], z_dev(d))
            for d in range(1, nz)
        ]
        for f in range(CHUNKS)
    ]

    def send_plane(f):
        at = slice(f * width, (f + 1) * width)
        for q in range(4):
            s1[f, q] = acc[q * rows:(q + 1) * rows, at].astype(jnp.bfloat16)
        for copy in a_copies[f]:
            copy.start()

    def send_z(f):
        at = slice(f * width, (f + 1) * width)
        total = acc[pl.ds(pl.multiple_of(plane * rows, rows), rows), at]
        for d in range(1, 4):
            a_copies[f][d - 1].wait_recv()
            total = total + r1[f, d - 1].astype(jnp.float32)
        stage[0:rows, at] = total
        for k in range(nz):
            mid[f, k] = stage[k * tokens:(k + 1) * tokens, at]
            s2[f, k] = mid[f, k].astype(jnp.bfloat16)
        for copy in b_copies[f]:
            copy.start()

    def store(f):
        at = slice(f * width, (f + 1) * width)
        total = mid[f, z]
        for d in range(1, nz):
            b_copies[f][d - 1].wait_recv()
            total = total + r2[f, d - 1].astype(jnp.float32)
        out_ref[:, at] = gx[plane, z, :, at].astype(jnp.float32) * total

    for j in range(tiles - 1):
        derive(j)
    acc[:, 0:width] = product(0, 0, tiles - 1)
    derive(tiles - 1)
    acc[:, 0:width] += product(0, tiles - 1, tiles)
    send_plane(0)
    for f in range(1, CHUNKS):
        acc[:, f * width:(f + 1) * width] = product(f, 0, tiles)
        send_plane(f)
        send_z(f - 1)
        if f > 1:
            store(f - 2)
    send_z(CHUNKS - 1)
    store(CHUNKS - 2)
    store(CHUNKS - 1)

    for copies in z_copies + p_copies[0] + p_copies[1] + [gu_moves, dn_moves] + a_copies + b_copies:
        for copy in copies:
            copy.wait_send()


def shared(nz, inputs, out_grads, w_gate, w_up, w_down):
    tokens, feats = inputs.shape
    half = w_gate.shape[1] // 2
    tiles = half // TILE
    width = feats // CHUNKS
    rows = nz * tokens
    every = 4 * rows
    f32, bf16 = jnp.float32, jnp.bfloat16
    dma = pltpu.SemaphoreType.DMA
    return pl.pallas_call(
        functools.partial(kernel, nz, tiles),
        out_shape=jax.ShapeDtypeStruct((tokens, feats), f32),
        in_specs=[pl.BlockSpec(memory_space=pl.ANY)] * 5,
        out_specs=pl.BlockSpec(memory_space=pltpu.VMEM),
        scratch_shapes=[
            pltpu.VMEM((feats, half), bf16),
            pltpu.VMEM((feats, half), bf16),
            pltpu.VMEM((half, feats), bf16),
            pltpu.VMEM((4, nz, tokens, feats), bf16),
            pltpu.VMEM((4, nz, tokens, feats), bf16),
            pltpu.VMEM((every, feats), f32),
            pltpu.VMEM((every, feats), bf16),
            pltpu.VMEM((every, feats), bf16),
            pltpu.VMEM((tiles, 2, every, TILE), f32),
            pltpu.VMEM((tiles, 2, every, TILE), f32),
            pltpu.VMEM((tiles, every, TILE), f32),
            pltpu.VMEM((tiles, every, TILE), f32),
            pltpu.VMEM((every, half), bf16),
            pltpu.VMEM((every, half), bf16),
            pltpu.VMEM((every, feats), f32),
            pltpu.VMEM((CHUNKS, 4, rows, width), bf16),
            pltpu.VMEM((CHUNKS, 3, rows, width), bf16),
            pltpu.VMEM((CHUNKS, nz, tokens, width), f32),
            pltpu.VMEM((CHUNKS, nz, tokens, width), bf16),
            pltpu.VMEM((CHUNKS, nz - 1, tokens, width), bf16),
            dma((3, tiles)), dma((2,)),
            dma((2, nz - 1)), dma((2, nz - 1)),
            dma((2, nz, 3)), dma((2, nz, 3)),
            dma((tiles,)), dma((tiles,)),
            dma((tiles,)), dma((tiles,)),
            dma((CHUNKS, 3)), dma((CHUNKS, 3)),
            dma((CHUNKS, nz - 1)), dma((CHUNKS, nz - 1)),
        ],
        compiler_params=pltpu.CompilerParams(
            collective_id=0, has_side_effects=True, vmem_limit_bytes=60 << 20
        ),
    )(inputs, out_grads, w_gate, w_up, w_down)


def solution(mesh):
    in_specs = (
        P(("groups", "row"), "col"),
        P(("groups", "row"), "col"),
        P("col", "row"),
        P("col", "row"),
        P("row", "col"),
    )
    out_specs = P(("groups", "row"), "col")
    groups, row, col = (mesh.shape[name] for name in ("groups", "row", "col"))

    def body(inputs, out_grads, w_gate, w_up, w_down):
        tokens, feats = inputs.shape
        nz = row // 2
        hidden = w_gate.shape[1]
        held = 3 * feats * hidden + 60 * groups * row * tokens * feats
        fits = (
            groups == 2 and col == 2 and row % 2 == 0 and nz > 1
            and hidden % (2 * TILE) == 0 and feats % (128 * CHUNKS) == 0 and hidden > 2 * TILE
            and nz * tokens == 8 and held < (56 << 20)
        )
        plan = functools.partial(shared, nz) if fits else per_device
        return plan(inputs, out_grads, w_gate, w_up, w_down)

    return jax.shard_map(
        body, mesh=mesh, in_specs=in_specs, out_specs=out_specs, check_vma=False
    )
```

time: 200 us -> 43.6 us (0.22)
  waiting for transfers between devices: 90.6 us -> 0 us
  matrix products: 58.6 us -> 0 us
  Pallas kernels: 0 us -> 42 us
  blocking collectives: 32.5 us -> 0 us
  between operations: 14.1 us -> 0.01 us
  other arithmetic: 3.21 us -> 0 us
    unnamed x3 -> x0, waiting for transfers between devices: 70.7 us -> none
    dot_general x5 -> x0, matrix products: 58.6 us -> none  [the longest x1 14.9 us: per_device(): lax.dot_general(derived[0], w_gate, (((1,), (1,)), ((), ())), preferred_e...]
    pallas_call x0 -> x1, Pallas kernels: none -> 42 us  [shared(): pl.pallas_call(functools.partial(kernel, nz, tiles), out_shape=jax.ShapeD...]
    all_gather x1 -> x0, blocking collectives: 32.5 us -> none  [per_device(): piece = lax.all_gather(stacked, 'row', axis=1, tiled=True)]
    psum x1 -> x0, waiting for transfers between devices: 19.9 us -> none  [per_device(): summed = lax.psum(partial_sums, 'col')]
  transfers between devices with their start and end apart: 2 -> 0, of which waited for: 2 -> 0; matrix products, arithmetic and copies ran while one was open for 0% -> 0% of each run, Pallas kernels for 0% -> 0%
where the time goes in v2:
time: 43.6 us; the launch traced here: 43.4 us
  Pallas kernels  42 us (96%)
  local copies, waits for them, and re-layouts  1.38 us (3%)
    pallas_call x1, Pallas kernels, shared(): pl.pallas_call(functools.partial(kernel, nz, tiles), out_shape=jax.ShapeD...  42 us
    unnamed x1, local copies, waits for them, and re-layouts  1.38 us

profile of v2, /device:TPU:0, one launch (start us, length us, event | category | flops | bytes accessed | tf_op | source)
XLA Modules:
  0.0 43.4 jit_solution(1285949425075385605)
XLA Ops:
  0.0 42.0 %shard_map.55 = f32[2,4096]{1,0:T(2,128)} custom-call(bf16[2,4096]{1,0:T(2,128)(2,1)} %in_hbm.1, bf16[2,4096]{1,0:T(2,128)(2,1)} %og_hbm.1, bf16[4096,3072]{1,0:T(8,128)(2,1)} %wg_hbm.1, bf16[4096,3072]{1,0:T(8,128)(2,1)} %wu_hbm.1, bf16[3072,4096]{1,0:T(8,128)(2,1)} %wd_hbm.1), custom_call_target="tpu_custom_call" | custom-call | tf_op jit(solution)/shard_map/pallas_call | solution.py:264
  42.0 1.4 %copy.7 = f32[2,4096]{1,0:T(2,128)} copy(f32[2,4096]{1,0:T(2,128)} %shard_map.55) | data formatting | bytes 65536
